TPU v7x, 512 devices: a whole 4x4x16 slice. The times are simulated.
512 devices in a mesh: node: 64 (over y, z), local: 8 (over x, core).
Axes of the slice: x: 4, y: 4, z: 16, core: 2. Of those that a mesh axis runs over, the one named last changes fastest.
Arguments:
- grad_out: bfloat16 [65536, 3584], P(('node', 'local')), may hold values from -6 to 6
- expert_ids: int32 [65536, 8], P(('node', 'local')), may hold values from 0 to 255, as said below
- gate_weights: float32 [65536, 8], P(('node', 'local')), may hold values from 0.05 to 0.35
- saved_hidden: bfloat16 [64, 1024, 1024], P('node', None, 'local'), may hold values from -0.59765625 to 0.59765625
- down_weight: bfloat16 [64, 1024, 3584], P('node', 'local'), may hold values from -0.1875 to 0.1875
- second_moment: bfloat16 [64, 1024, 3584], P('node', 'local'), may hold values from 0.0019989014 to 0.25
Outputs:
- gate_weight_gradient: float32 [65536, 8], P(('node', 'local'))
- hidden_grad: bfloat16 [64, 1024, 1024], P('node', None, 'local')
- new_weight: bfloat16 [64, 1024, 3584], P('node', 'local')
- new_second: bfloat16 [64, 1024, 3584], P('node', 'local')
Inputs may be any that keep to these rules, and one draw needn't show every extreme that they name: `expert_ids`: each row names 8 different experts on at most 4 nodes (node = id // 4), two on each; at most one per row is in flight (id % 4 == 0). Among the rows of one device at most 2 name the in-flight expert of any one node, and in every draw some node receives exactly 2 from every device.
All inputs are finite; a program needn't handle non-finite values.
Results may differ from a plain program's by a relative error of at most 0.0051.
Values may be sent and summed in bfloat16 or wider, within the bound.
No kernel may reach another device: no remote copies, remote signals or barrier semaphores. Data moves between devices by JAX's collectives and lax.ppermute only.
A program may use at most 128 MiB of HBM per device.

v0:
```python
import jax
import jax.numpy as jnp
from jax import lax
from jax.sharding import PartitionSpec as P

EXPERTS_PER_HOST = 4
CAP = 2
beta_second = 0.95
learn_rate = 0.002
decay_rate = 0.1
epsilon = 1e-08
correct_second = 0.994079470779666


def gather_rows(picked_experts, gate_values, grads, node_count):
    transit_rows = picked_experts % EXPERTS_PER_HOST == 0
    row_present = jnp.any(transit_rows, 1)
    destination_node = jnp.sum(jnp.where(transit_rows, picked_experts // EXPERTS_PER_HOST, 0), 1)
    onehot = (
        (destination_node[:, None] == jnp.arange(node_count, dtype=jnp.int32)[None, :])
        & row_present[:, None]
    ).astype(jnp.int32)
    within_rank = jnp.sum(onehot * (jnp.cumsum(onehot, 0) - 1), 1)
    slot_index = destination_node * CAP + within_rank
    expert_location = (
        jnp.arange(node_count * CAP, dtype=jnp.int32)[:, None] == slot_index[None, :]
    ) & row_present[None, :]
    matched_gate = jnp.sum(jnp.where(transit_rows, gate_values, 0.0), 1).astype(jnp.bfloat16)
    departing_rows = jnp.dot(
        expert_location.astype(jnp.bfloat16), grads, preferred_element_type=jnp.float32
    ).astype(jnp.bfloat16)
    departing_gates = jnp.sum(
        jnp.where(expert_location, matched_gate.astype(jnp.float32)[None, :], 0.0), 1
    ).astype(jnp.bfloat16)
    feature_count = grads.shape[1]
    return (
        departing_rows.reshape(node_count, CAP, feature_count),
        departing_gates.reshape(node_count, CAP),
        expert_location,
        transit_rows,
    )


def on_device(grad_out, expert_ids, gate_weights, saved_hidden, down_weight, second_moment):
    node_count = lax.axis_size("node")
    members = lax.axis_size("local")
    feature_count = grad_out.shape[1]
    departing_rows, departing_gates, expert_location, transit_rows = gather_rows(
        expert_ids, gate_weights, grad_out, node_count
    )
    copies, copy_gates = (
        lax.all_gather(departing_rows[None], "local", axis=0, tiled=True),
        lax.all_gather(departing_gates[None], "local", axis=0, tiled=True),
    )
    arrived, arrived_gates = (
        lax.all_to_all(copies, "node", split_axis=1, concat_axis=1, tiled=True),
        lax.all_to_all(copy_gates, "node", split_axis=1, concat_axis=1, tiled=True),
    )
    arrived_rows = arrived.reshape(-1, feature_count)
    slot_gates = arrived_gates.reshape(-1).astype(jnp.float32)
    weight_now = down_weight[0]
    hidden_now = saved_hidden[0]
    unscaled = lax.dot_general(
        arrived_rows, weight_now, (((1,), (1,)), ((), ())), preferred_element_type=jnp.float32
    )
    hidden_out = (slot_gates[:, None] * unscaled).astype(jnp.bfloat16)
    slot_score = jnp.sum(unscaled * hidden_now.astype(jnp.float32), 1)
    scaled = (slot_gates[:, None] * arrived_rows.astype(jnp.float32)).astype(jnp.bfloat16)
    grad = lax.dot_general(
        hidden_now, scaled, (((0,), (0,)), ((), ())), preferred_element_type=jnp.float32
    )
    second_new = (
        beta_second * second_moment[0].astype(jnp.float32) + (1.0 - beta_second) * grad * grad
    )
    weight_f = weight_now.astype(jnp.float32)
    update = grad / (jnp.sqrt(second_new / correct_second) + epsilon) + decay_rate * weight_f
    weight_new = weight_f - learn_rate * update
    score_terms = slot_score.reshape(members, node_count * CAP)
    summed = lax.psum(score_terms, "local")
    own_terms = lax.dynamic_slice_in_dim(summed, lax.axis_index("local"), 1, 0)
    returned = lax.all_to_all(
        own_terms.reshape(node_count, CAP), "node", split_axis=0, concat_axis=0, tiled=True
    )
    returned_flat = returned.reshape(node_count * CAP)
    token_gradient = jnp.sum(jnp.where(expert_location, returned_flat[:, None], 0.0), 0)
    gate_weight_gradient = jnp.where(transit_rows, token_gradient[:, None], 0.0)
    return (
        gate_weight_gradient,
        hidden_out[None],
        weight_new.astype(jnp.bfloat16)[None],
        second_new.astype(jnp.bfloat16)[None],
    )


def solution(mesh):
    return jax.shard_map(
        on_device,
        mesh=mesh,
        in_specs=(
            P(("node", "local"), None),
            P(("node", "local"), None),
            P(("node", "local"), None),
            P("node", None, "local"),
            P("node", "local", None),
            P("node", "local", None),
        ),
        out_specs=(
            P(("node", "local"), None),
            P("node", None, "local"),
            P("node", "local", None),
            P("node", "local", None),
        ),
        check_vma=False,
    )
```

profile of v0, /device:TPU:2, one launch (start us, length us, event | category | flops | bytes accessed | tf_op | source)
XLA Modules:
  0.0 566.0 jit_solution(3273625820910826075)
XLA Ops:
  7.2 0.0 copy-start
  7.2 0.0 all-gather.2.cloned.1.call-start
  7.2 0.8 fusion.22
  8.0 0.7 fusion.19
  8.7 0.1 fusion.14
  8.8 0.2 reduce_window_sum.11
  9.0 0.2 select_reduce_fusion.2
  9.2 0.0 copy-done
  9.2 0.4 convolution_convert_fusion
  9.6 0.3 broadcast_in_dim_reshape.2
  9.9 1.0 copy.65
  11.0 0.0 all-gather.2.cloned.1.call-update
  11.0 56.7 %all-gather.2.cloned.1.call-done = bf16[8,64,2,3584]{3,1,2,0:T(8,128)(2,1)} async-done(((bf16[1,64,2,3584]{3,1,2,0:T(8,128)(2,1)}), bf16[8,64,2,3584]{3,1,2,0:T(8,128)(2,1)}) %all-gather.2.cloned.1.call-update) | async-done | bytes 7340048 | tf_op jit(solution)/shard_map/all_gather | solution.py:52
  67.7 14.7 %copy.66 = bf16[8,64,2,3584]{3,2,0,1:T(2,128)(2,1)} copy(bf16[8,64,2,3584]{3,1,2,0:T(8,128)(2,1)} %all-gather.2.cloned.1.call-done) | data formatting | bytes 14680064 | tf_op jit(solution)/shard_map/all_gather | solution.py:52
  82.4 0.0 copy-start.5
  82.4 16.0 %all-to-all-start = ((bf16[8,64,2,3584]{3,2,0,1:T(2,128)(2,1)}), bf16[8,64,2,3584]{3,2,0,1:T(2,128)(2,1)}, u32[]{:S(2)}, u32[]{:S(2)}) async-start(bf16[8,64,2,3584]{3,2,0,1:T(2,128)(2,1)} %copy.66), calls=%async_computation | async-start | bytes 14680064 | tf_op jit(solution)/shard_map/all_to_all | solution.py:56
  98.4 0.0 copy-done.5
  98.4 0.1 copy.69
  98.6 323.8 %all-to-all-done = bf16[8,64,2,3584]{3,2,0,1:T(2,128)(2,1)} async-done(((bf16[8,64,2,3584]{3,2,0,1:T(2,128)(2,1)}), bf16[8,64,2,3584]{3,2,0,1:T(2,128)(2,1)}, u32[]{:S(2)}, u32[]{:S(2)}) %all-to-all-start) | async-done | bytes 7340064 | tf_op jit(solution)/shard_map/all_to_all | solution.py:56
  422.4 7.4 %copy.67 = bf16[8,64,2,3584]{3,2,1,0:T(2,128)(2,1)} copy(bf16[8,64,2,3584]{3,2,0,1:T(2,128)(2,1)} %all-to-all-done) | data formatting | bytes 14680064 | tf_op jit(solution)/shard_map/all_to_all | solution.py:56
  429.8 0.0 copy-start.2
  429.8 15.5 %reshape.62 = bf16[1024,3584]{1,0:T(8,128)(2,1)} reshape(bf16[8,64,2,3584]{3,2,1,0:T(2,128)(2,1)} %copy.67) | data formatting | bytes 14680064 | tf_op jit(solution)/shard_map/reshape | solution.py:59
  445.4 0.0 copy-done.2
  445.4 0.0 copy-start.6
  445.4 5.6 multiply_reduce_fusion
  450.9 0.0 copy-start.3
  451.0 10.5 %psum.7 = f32[8,128]{1,0:T(8,128)S(1)} all-reduce(f32[8,128]{1,0:T(8,128)S(1)} %bitcast.41), channel_id=1, replica_groups=mesh['node'=64,'local'=8] {'local'}, use_global_device_ids=true, to_apply=%region_5.6 | all-reduce | flops 1024 | bytes 8192 | tf_op jit(solution)/shard_map/psum | solution.py:79
  461.5 0.8 all_to_all.13
  462.2 7.0 %all-to-all-start.1 = ((f32[64,1,2]{2,1,0:T(1,128)}), f32[64,1,2]{2,1,0:T(1,128)}, u32[]{:S(2)}, u32[]{:S(2)}) async-start(f32[64,1,2]{2,1,0:T(1,128)} %bitcast.3), calls=%async_computation.1 | async-start | bytes 65536 | tf_op jit(solution)/shard_map/all_to_all | solution.py:81
  469.2 0.0 copy-done.6
  469.2 0.5 select_reduce_fusion.3
  469.8 0.6 copy.68
  470.4 0.7 convert_element_type.132
  471.1 0.0 copy-done.3
  471.1 0.6 copy.78
  471.7 11.6 %all-to-all-done.1 = f32[64,1,2]{2,1,0:T(1,128)} async-done(((f32[64,1,2]{2,1,0:T(1,128)}), f32[64,1,2]{2,1,0:T(1,128)}, u32[]{:S(2)}, u32[]{:S(2)}) %all-to-all-start.1) | async-done | bytes 544 | tf_op jit(solution)/shard_map/all_to_all | solution.py:81
  483.3 0.5 broadcast.47
  483.8 1.5 reduce.7
  485.3 0.1 broadcast_in_dim.59
  485.4 0.1 select_reduce_fusion
  485.6 0.2 convert_element_type.82
  485.7 0.1 copy.71
  485.8 11.1 %all_gather.7 = bf16[8,64,2]{1,2,0:T(2,128)(2,1)S(1)} all-gather(bf16[1,64,2]{1,2,0:T(2,128)(2,1)S(1)} %copy.71), channel_id=1, replica_groups=mesh['node'=64,'local'=8] {'local'}, dimensions={0}, use_global_device_ids=true | all-gather | bytes 2304 | tf_op jit(solution)/shard_map/all_gather | solution.py:53
  496.9 0.7 copy.72
  497.6 4.8 all-to-all-start.2
  502.4 0.6 broadcast_select_fusion
  503.0 13.6 %all-to-all-done.2 = bf16[8,64,2]{0,2,1:T(2,128)(2,1)S(1)} async-done(((bf16[8,64,2]{0,2,1:T(2,128)(2,1)}), bf16[8,64,2]{0,2,1:T(2,128)(2,1)S(1)}, u32[]{:S(2)}, u32[]{:S(2)}) %all-to-all-start.2) | async-done | bytes 2080 | tf_op jit(solution)/shard_map/all_to_all | solution.py:57
  516.6 0.1 copy.73
  516.7 0.2 copy.74
  516.8 7.8 %multiply_convert_fusion = bf16[8,64,2,3584]{3,1,2,0:T(8,128)(2,1)S(1)} fusion(bf16[8,64,2,3584]{3,2,0,1:T(2,128)(2,1)} %all-to-all-done, f32[8,64,2]{1,2,0:T(2,128)S(1)} %copy.75), kind=kLoop, calls=%fused_computation | loop fusion | flops 11010048 | bytes 14684160 | tf_op jit(solution)/shard_map/convert_element_type | solution.py:68
  524.6 7.1 %copy.77 = bf16[8,64,2,3584]{3,2,1,0:T(2,128)(2,1)} copy(bf16[8,64,2,3584]{3,1,2,0:T(8,128)(2,1)S(1)} %multiply_convert_fusion) | data formatting | bytes 14680064 | tf_op jit(solution)/shard_map/convert_element_type | solution.py:68
  531.7 15.4 %convert_element_type.90 = bf16[1024,3584]{1,0:T(8,128)(2,1)} reshape(bf16[8,64,2,3584]{3,2,1,0:T(2,128)(2,1)} %copy.77) | data formatting | bytes 14680064 | tf_op jit(solution)/shard_map/convert_element_type | solution.py:68
  547.1 7.3 %fusion.5 = (bf16[1,128,3584]{1,2,0:T(8,128)(2,1)}, bf16[1,128,3584]{1,2,0:T(8,128)(2,1)}) fusion(bf16[1,128,3584]{1,2,0:T(8,128)(2,1)S(1)} %copy.78, bf16[1,128,3584]{1,2,0:T(8,128)(2,1)S(1)} %copy.68, bf16[1024,3584]{1,0:T(8,128)(2,1)} %convert_element_type.90, bf16[1,1024,128]{2,1,0:T(8,128)(2,1)S(1)} %copy-done.5), kind=kOutput, calls=%fused_computation.11 | convolution fusion | flops 946405376 | bytes 11272192 | tf_op jit(solution)/shard_map/dot_general | solution.py:69
  554.5 0.0 copy-start.4
  554.5 0.0 copy-start.1
  554.5 2.3 copy.80
  556.8 0.0 copy-done.4
  556.8 1.3 copy.81
  558.1 0.2 reshape.64
  558.3 0.8 copy.79
  559.1 0.0 copy-done.1
  (4 shorter events, 0.1 us)
Async XLA Ops:
  7.2 2.0 copy-start
  7.2 60.5 %all-gather.2.cloned.1.call-start = ((), (), s32[]{:S(2)}) async-start(), calls=%async_computation.3 | async-start | bytes 8257536 | tf_op jit(solution)/shard_map/all_gather | solution.py:52
  82.4 16.0 %copy-start.5 = (bf16[1,1024,128]{2,1,0:T(8,128)(2,1)S(1)}, bf16[1,1024,128]{2,1,0:T(8,128)(2,1)}, u32[]{:S(2)}) copy-start(bf16[1,1024,128]{2,1,0:T(8,128)(2,1)} %param.9) | copy-start | bytes 786436
  82.4 340.0 %all-to-all-start = ((bf16[8,64,2,3584]{3,2,0,1:T(2,128)(2,1)}), bf16[8,64,2,3584]{3,2,0,1:T(2,128)(2,1)}, u32[]{:S(2)}, u32[]{:S(2)}) async-start(bf16[8,64,2,3584]{3,2,0,1:T(2,128)(2,1)} %copy.66), calls=%async_computation | async-start | bytes 14680064 | tf_op jit(solution)/shard_map/all_to_all | solution.py:56
  429.8 15.5 %copy-start.2 = (bf16[1,128,3584]{2,1,0:T(8,128)(2,1)S(1)}, bf16[1,128,3584]{2,1,0:T(8,128)(2,1)}, u32[]{:S(2)}) copy-start(bf16[1,128,3584]{2,1,0:T(8,128)(2,1)} %param.10) | copy-start | bytes 2752516
  445.4 23.9 %copy-start.6 = (f32[128,8]{0,1:T(8,128)S(1)}, f32[128,8]{0,1:T(8,128)}, u32[]{:S(2)}) copy-start(f32[128,8]{0,1:T(8,128)} %param.8) | copy-start | bytes 12292
  450.9 20.1 %copy-start.3 = (bf16[1,128,3584]{2,1,0:T(8,128)(2,1)S(1)}, bf16[1,128,3584]{2,1,0:T(8,128)(2,1)}, u32[]{:S(2)}) copy-start(bf16[1,128,3584]{2,1,0:T(8,128)(2,1)} %param.11) | copy-start | bytes 2752516
  462.2 21.0 %all-to-all-start.1 = ((f32[64,1,2]{2,1,0:T(1,128)}), f32[64,1,2]{2,1,0:T(1,128)}, u32[]{:S(2)}, u32[]{:S(2)}) async-start(f32[64,1,2]{2,1,0:T(1,128)} %bitcast.3), calls=%async_computation.1 | async-start | bytes 65536 | tf_op jit(solution)/shard_map/all_to_all | solution.py:81
  497.6 19.0 %all-to-all-start.2 = ((bf16[8,64,2]{0,2,1:T(2,128)(2,1)}), bf16[8,64,2]{0,2,1:T(2,128)(2,1)S(1)}, u32[]{:S(2)}, u32[]{:S(2)}) async-start(bf16[8,64,2]{0,2,1:T(2,128)(2,1)} %copy.72), calls=%async_computation.2 | async-start | bytes 65536 | tf_op jit(solution)/shard_map/all_to_all | solution.py:57
  554.5 2.4 copy-start.4
  554.5 4.7 copy-start.1
Sparse Core Ops, SparseCore 0:
  11.1 56.5 all-gather.1
where the time goes:
time: 567 us; the launch traced here: 566 us
  waiting for transfers between devices  406 us (72%)
  local copies, waits for them, and re-layouts  70.1 us (12%)
  starting transfers between devices  27.8 us (5%)
  blocking collectives  21.6 us (4%)
  between operations  14.2 us (3%)
  matrix products  13.3 us (2%)
  other arithmetic  13.2 us (2%)
    all_to_all x1, waiting for transfers between devices, on_device(): lax.all_to_all(copies, 'node', split_axis=1, concat_axis=1, tiled=True)  324 us
    all_gather x1, waiting for transfers between devices, on_device(): lax.all_gather(departing_rows[None], 'local', axis=0, tiled=True)  56.7 us
    convert_element_type x2, local copies, waits for them, and re-layouts, on_device(): (slot_gates[:, None] * arrived_rows.astype(jnp.float32)).astype(jnp.bfloa...  22.5 us
    all_to_all x1, starting transfers between devices, on_device(): lax.all_to_all(copies, 'node', split_axis=1, concat_axis=1, tiled=True)  16 us
    reshape x1, local copies, waits for them, and re-layouts, on_device(): arrived_rows = arrived.reshape(-1, feature_count)  15.5 us
    all_gather x1, local copies, waits for them, and re-layouts, on_device(): lax.all_gather(departing_rows[None], 'local', axis=0, tiled=True)  14.7 us
    all_to_all x1, waiting for transfers between devices, on_device(): lax.all_to_all(copy_gates, 'node', split_axis=1, concat_axis=1, tiled=True)  13.6 us
    all_to_all x1, waiting for transfers between devices, on_device(): lax.all_to_all(own_terms.reshape(node_count, CAP), 'node', split_axis=0,...  11.6 us
  transfers between devices with their start and end apart: 4, of which 4 were waited for; matrix products, arithmetic and copies ran while one was open for 1% of the time, Pallas kernels for 0%

commit v1 on v0

--- a/solution.py
+++ b/solution.py
@@ -53,7 +53,12 @@
         lax.all_gather(departing_gates[None], "local", axis=0, tiled=True),
     )
     arrived, arrived_gates = (
-        lax.all_to_all(copies, "node", split_axis=1, concat_axis=1, tiled=True),
+        jnp.concatenate(
+            lax.all_to_all(
+                jnp.stack(jnp.split(copies, lax.axis_size("node"), axis=1)), "node", 0, 0
+            ),
+            axis=1,
+        ),
         lax.all_to_all(copy_gates, "node", split_axis=1, concat_axis=1, tiled=True),
     )
     arrived_rows = arrived.reshape(-1, feature_count)

time: 567 us -> 665 us (1.17)
  local copies, waits for them, and re-layouts: 70.1 us -> 167 us
    unnamed x20 -> x81, local copies, waits for them, and re-layouts: 5.85 us -> 110 us
    another operation x0 -> x2, local copies, waits for them, and re-layouts: none -> 17.2 us  [the longest x1 15.5 us: on_device(): arrived_rows = arrived.reshape(-1, feature_count)]
    all_gather x1 -> x0, local copies, waits for them, and re-layouts: 14.7 us -> none  [on_device(): lax.all_gather(departing_rows[None], 'local', axis=0, tiled=True)]
    reshape x1, local copies, waits for them, and re-layouts: 15.5 us -> 7.06 us  [on_device(): jnp.concatenate(lax.all_to_all(jnp.stack(jnp.split(copies, lax.axis_size(...]
  transfers between devices with their start and end apart: 4 -> 4, of which waited for: 4 -> 4; matrix products, arithmetic and copies ran while one was open for 1% -> 0% of each run, Pallas kernels for 0% -> 0%
where the time goes in v1:
time: 665 us; the launch traced here: 663 us
  waiting for transfers between devices  406 us (61%)
  local copies, waits for them, and re-layouts  167 us (25%)
  starting transfers between devices  28 us (4%)
  blocking collectives  21.5 us (3%)
  between operations  14.2 us (2%)
  matrix products  13.6 us (2%)
  other arithmetic  12 us (2%)
    all_to_all x1, waiting for transfers between devices, on_device(): lax.all_to_all(jnp.stack(jnp.split(copies, lax.axis_size('node'), axis=1)...  324 us
    unnamed x81, local copies, waits for them, and re-layouts  110 us
    all_gather x1, waiting for transfers between devices, on_device(): lax.all_gather(departing_rows[None], 'local', axis=0, tiled=True)  56.7 us
    convert_element_type x2, local copies, waits for them, and re-layouts, on_device(): (slot_gates[:, None] * arrived_rows.astype(jnp.float32)).astype(jnp.bfloa...  22.5 us
    all_to_all x1, starting transfers between devices, on_device(): lax.all_to_all(jnp.stack(jnp.split(copies, lax.axis_size('node'), axis=1)...  16.2 us
    another operation x1, local copies, waits for them, and re-layouts, on_device(): arrived_rows = arrived.reshape(-1, feature_count)  15.5 us
    all_to_all x1, waiting for transfers between devices, on_device(): lax.all_to_all(copy_gates, 'node', split_axis=1, concat_axis=1, tiled=True)  13.6 us
  transfers between devices with their start and end apart: 4, of which 4 were waited for; matrix products, arithmetic and copies ran while one was open for 0% of the time, Pallas kernels for 0%

profile of v1, /device:TPU:2, one launch (start us, length us, event | category | flops | bytes accessed | tf_op | source)
XLA Modules:
  0.0 662.8 jit_solution(13295500259745819986)
XLA Ops:
  10.9 56.7 %all-gather.2.cloned.1.call-done = bf16[8,64,2,3584]{3,2,0,1:T(2,128)(2,1)} async-done(((bf16[1,64,2,3584]{3,2,0,1:T(2,128)(2,1)}), bf16[8,64,2,3584]{3,2,0,1:T(2,128)(2,1)}) %all-gather.2.cloned.1.call-update) | async-done | bytes 7340048 | tf_op jit(solution)/shard_map/all_gather | solution.py:52
  67.6 1.6 constant_dynamic-update-slice_fusion.63
  70.8 1.6 constant_dynamic-update-slice_fusion.61
  75.7 1.6 constant_dynamic-update-slice_fusion.58
  77.3 1.6 constant_dynamic-update-slice_fusion.57
  80.6 1.6 constant_dynamic-update-slice_fusion.55
  82.2 1.7 constant_dynamic-update-slice_fusion.54
  85.5 1.6 constant_dynamic-update-slice_fusion.52
  87.1 1.6 constant_dynamic-update-slice_fusion.51
  90.3 1.6 constant_dynamic-update-slice_fusion.49
  91.9 1.6 constant_dynamic-update-slice_fusion.48
  93.6 1.6 constant_dynamic-update-slice_fusion.47
  95.2 1.6 constant_dynamic-update-slice_fusion.46
  100.1 1.6 constant_dynamic-update-slice_fusion.43
  101.7 1.6 constant_dynamic-update-slice_fusion.42
  103.3 1.6 constant_dynamic-update-slice_fusion.41
  108.2 1.6 constant_dynamic-update-slice_fusion.38
  111.4 1.6 constant_dynamic-update-slice_fusion.36
  113.0 1.6 constant_dynamic-update-slice_fusion.35
  114.7 1.6 constant_dynamic-update-slice_fusion.34
  116.3 1.6 constant_dynamic-update-slice_fusion.33
  117.9 1.6 constant_dynamic-update-slice_fusion.32
  119.5 1.6 constant_dynamic-update-slice_fusion.31
  121.2 1.6 constant_dynamic-update-slice_fusion.30
  124.4 1.6 constant_dynamic-update-slice_fusion.28
  126.0 1.6 constant_dynamic-update-slice_fusion.27
  129.3 1.6 constant_dynamic-update-slice_fusion.25
  134.1 1.6 constant_dynamic-update-slice_fusion.22
  135.7 1.6 constant_dynamic-update-slice_fusion.21
  137.4 1.6 constant_dynamic-update-slice_fusion.20
  139.0 1.6 constant_dynamic-update-slice_fusion.19
  140.6 1.6 constant_dynamic-update-slice_fusion.18
  142.3 1.6 constant_dynamic-update-slice_fusion.17
  147.1 1.6 constant_dynamic-update-slice_fusion.14
  148.8 1.6 constant_dynamic-update-slice_fusion.13
  150.4 1.6 constant_dynamic-update-slice_fusion.12
  152.0 1.6 constant_dynamic-update-slice_fusion.11
  153.6 1.6 constant_dynamic-update-slice_fusion.10
  155.3 1.6 constant_dynamic-update-slice_fusion.9
  156.9 1.6 constant_dynamic-update-slice_fusion.8
  158.5 1.6 constant_dynamic-update-slice_fusion.7
  160.1 1.6 constant_dynamic-update-slice_fusion.6
  163.4 1.6 constant_dynamic-update-slice_fusion.4
  165.0 1.6 constant_dynamic-update-slice_fusion.3
  166.6 1.6 constant_dynamic-update-slice_fusion.2
  168.2 1.6 constant_dynamic-update-slice_fusion.1
  171.5 16.2 %all-to-all-start = ((bf16[64,8,1,2,3584]{4,3,1,2,0:T(2,128)(2,1)}), bf16[64,8,1,2,3584]{4,3,1,2,0:T(2,128)(2,1)}, u32[]{:S(2)}, u32[]{:S(2)}) async-start(bf16[64,8,1,2,3584]{4,3,1,2,0:T(2,128)(2,1)} %constant_dynamic-update-slice_fusion), calls=%async_computation | async-start | bytes 14680064 | tf_op jit(solution)/shard_map/all_to_all | solution.py:57
  187.9 323.7 %all-to-all-done = bf16[64,8,1,2,3584]{4,3,1,2,0:T(2,128)(2,1)} async-done(((bf16[64,8,1,2,3584]{4,3,1,2,0:T(2,128)(2,1)}), bf16[64,8,1,2,3584]{4,3,1,2,0:T(2,128)(2,1)}, u32[]{:S(2)}, u32[]{:S(2)}) %all-to-all-start) | async-done | bytes 7340064 | tf_op jit(solution)/shard_map/all_to_all | solution.py:57
  511.5 7.1 %copy.197 = bf16[64,8,1,2,3584]{4,0,3,2,1:T(8,128)(2,1)S(1)} copy(bf16[64,8,1,2,3584]{4,3,1,2,0:T(2,128)(2,1)} %all-to-all-done) | data formatting | bytes 14680064 | tf_op jit(solution)/shard_map/all_to_all | solution.py:57
  518.6 7.1 %copy.180 = bf16[8,64,1,2,3584]{4,3,1,0,2:T(2,128)(2,1)} copy(bf16[8,64,1,2,3584]{4,1,3,2,0:T(8,128)(2,1)S(1)} %bitcast.307) | data formatting | bytes 14680064 | tf_op jit(solution)/shard_map/reshape | solution.py:56
  525.7 15.5 %reshape_reshape.3 = bf16[1024,3584]{1,0:T(8,128)(2,1)} reshape(bf16[8,64,1,2,3584]{4,3,1,0,2:T(2,128)(2,1)} %copy.180) | data formatting | bytes 14680064 | tf_op jit(solution)/shard_map/reshape;reshape | solution.py:64
  541.2 5.6 multiply_reduce_fusion
  546.8 10.4 %psum.7 = f32[8,128]{1,0:T(8,128)S(1)} all-reduce(f32[8,128]{1,0:T(8,128)S(1)} %bitcast.309), channel_id=1, replica_groups=mesh['node'=64,'local'=8] {'local'}, use_global_device_ids=true, to_apply=%region_5.6 | all-reduce | flops 1024 | bytes 8192 | tf_op jit(solution)/shard_map/psum | solution.py:84
  558.0 7.0 %all-to-all-start.1 = ((f32[64,1,2]{2,1,0:T(1,128)}), f32[64,1,2]{2,1,0:T(1,128)}, u32[]{:S(2)}, u32[]{:S(2)}) async-start(f32[64,1,2]{2,1,0:T(1,128)} %bitcast.69), calls=%async_computation.1 | async-start | bytes 65536 | tf_op jit(solution)/shard_map/all_to_all | solution.py:86
  566.9 12.1 %all-to-all-done.1 = f32[64,1,2]{2,1,0:T(1,128)} async-done(((f32[64,1,2]{2,1,0:T(1,128)}), f32[64,1,2]{2,1,0:T(1,128)}, u32[]{:S(2)}, u32[]{:S(2)}) %all-to-all-start.1) | async-done | bytes 544 | tf_op jit(solution)/shard_map/all_to_all | solution.py:86
  581.5 11.1 %all_gather.7 = bf16[8,64,2]{1,2,0:T(2,128)(2,1)S(1)} all-gather(bf16[1,64,2]{1,2,0:T(2,128)(2,1)S(1)} %copy.184), channel_id=1, replica_groups=mesh['node'=64,'local'=8] {'local'}, dimensions={0}, use_global_device_ids=true | all-gather | bytes 2304 | tf_op jit(solution)/shard_map/all_gather | solution.py:53
  593.4 4.8 all-to-all-start.2
  598.8 13.6 %all-to-all-done.2 = bf16[8,64,2]{0,2,1:T(2,128)(2,1)S(1)} async-done(((bf16[8,64,2]{0,2,1:T(2,128)(2,1)}), bf16[8,64,2]{0,2,1:T(2,128)(2,1)S(1)}, u32[]{:S(2)}, u32[]{:S(2)}) %all-to-all-start.2) | async-done | bytes 2080 | tf_op jit(solution)/shard_map/all_to_all | solution.py:62
  612.6 7.8 %multiply_convert_fusion = bf16[8,64,1,2,3584]{4,1,3,2,0:T(8,128)(2,1)S(1)} fusion(f32[8,64,2]{1,2,0:T(2,128)S(1)} %copy.188, bf16[64,8,1,2,3584]{4,3,1,2,0:T(2,128)(2,1)} %all-to-all-done), kind=kLoop, calls=%fused_computation | loop fusion | flops 11010048 | bytes 14684160 | tf_op jit(solution)/shard_map/convert_element_type | solution.py:73
  620.4 7.1 %copy.189 = bf16[8,64,1,2,3584]{4,3,1,0,2:T(2,128)(2,1)} copy(bf16[8,64,1,2,3584]{4,1,3,2,0:T(8,128)(2,1)S(1)} %multiply_convert_fusion) | data formatting | bytes 14680064 | tf_op jit(solution)/shard_map/convert_element_type | solution.py:73
  627.4 15.4 %convert_element_type.90 = bf16[1024,3584]{1,0:T(8,128)(2,1)} reshape(bf16[8,64,1,2,3584]{4,3,1,0,2:T(2,128)(2,1)} %copy.189) | data formatting | bytes 14680064 | tf_op jit(solution)/shard_map/convert_element_type | solution.py:73
  642.9 7.6 %fusion.5 = (bf16[1,128,3584]{1,2,0:T(8,128)(2,1)}, bf16[1,128,3584]{1,2,0:T(8,128)(2,1)}) fusion(bf16[1,128,3584]{1,2,0:T(8,128)(2,1)} %copy.190, bf16[1,128,3584]{1,2,0:T(8,128)(2,1)S(1)} %copy.181, bf16[1024,3584]{1,0:T(8,128)(2,1)} %convert_element_type.90, bf16[1,1024,128]{2,1,0:T(8,128)(2,1)S(1)} %copy-done.4), kind=kOutput, calls=%fused_computation.12 | convolution fusion | flops 946405376 | bytes 11272192 | tf_op jit(solution)/shard_map/dot_general | solution.py:74
  650.5 2.2 copy.192
  652.7 2.2 copy.193
  (62 shorter events, 42.3 us)
Async XLA Ops:
  7.2 2.0 copy-start
  7.2 60.4 %all-gather.2.cloned.1.call-start = ((), (), s32[]{:S(2)}) async-start(), calls=%async_computation.3 | async-start | bytes 8257536 | tf_op jit(solution)/shard_map/all_gather | solution.py:52
  171.5 16.2 %copy-start.4 = (bf16[1,1024,128]{2,1,0:T(8,128)(2,1)S(1)}, bf16[1,1024,128]{2,1,0:T(8,128)(2,1)}, u32[]{:S(2)}) copy-start(bf16[1,1024,128]{2,1,0:T(8,128)(2,1)} %param.9) | copy-start | bytes 786436
  171.5 340.0 %all-to-all-start = ((bf16[64,8,1,2,3584]{4,3,1,2,0:T(2,128)(2,1)}), bf16[64,8,1,2,3584]{4,3,1,2,0:T(2,128)(2,1)}, u32[]{:S(2)}, u32[]{:S(2)}) async-start(bf16[64,8,1,2,3584]{4,3,1,2,0:T(2,128)(2,1)} %constant_dynamic-update-slice_fusion), calls=%async_computation | async-start | bytes 14680064 | tf_op jit(solution)/shard_map/all_to_all | solution.py:57
  525.7 15.5 %copy-start.2 = (bf16[1,128,3584]{2,1,0:T(8,128)(2,1)S(1)}, bf16[1,128,3584]{2,1,0:T(8,128)(2,1)}, u32[]{:S(2)}) copy-start(bf16[1,128,3584]{2,1,0:T(8,128)(2,1)} %param.10) | copy-start | bytes 2752516
  541.2 23.8 %copy-start.5 = (f32[128,8]{0,1:T(8,128)S(1)}, f32[128,8]{0,1:T(8,128)}, u32[]{:S(2)}) copy-start(f32[128,8]{0,1:T(8,128)} %param.8) | copy-start | bytes 12292
  541.2 24.4 %copy-start.3 = (bf16[1,128,3584]{2,1,0:T(8,128)(2,1)S(1)}, bf16[1,128,3584]{2,1,0:T(8,128)(2,1)}, u32[]{:S(2)}) copy-start(bf16[1,128,3584]{2,1,0:T(8,128)(2,1)} %param.11) | copy-start | bytes 2752516
  558.0 21.0 %all-to-all-start.1 = ((f32[64,1,2]{2,1,0:T(1,128)}), f32[64,1,2]{2,1,0:T(1,128)}, u32[]{:S(2)}, u32[]{:S(2)}) async-start(f32[64,1,2]{2,1,0:T(1,128)} %bitcast.69), calls=%async_computation.1 | async-start | bytes 65536 | tf_op jit(solution)/shard_map/all_to_all | solution.py:86
  593.4 19.0 %all-to-all-start.2 = ((bf16[8,64,2]{0,2,1:T(2,128)(2,1)}), bf16[8,64,2]{0,2,1:T(2,128)(2,1)S(1)}, u32[]{:S(2)}, u32[]{:S(2)}) async-start(bf16[8,64,2]{0,2,1:T(2,128)(2,1)} %copy.185), calls=%async_computation.2 | async-start | bytes 65536 | tf_op jit(solution)/shard_map/all_to_all | solution.py:62
  642.9 13.1 %copy-start.1 = (bf16[128,3584]{1,0:T(8,128)(2,1)S(1)}, bf16[128,3584]{1,0:T(8,128)(2,1)}, u32[]{:S(2)}) copy-start(bf16[128,3584]{1,0:T(8,128)(2,1)} %param.6) | copy-start | bytes 2752516
Sparse Core Ops, SparseCore 0:
  11.0 56.5 all-gather.1
